TPU v7x, 32 devices: a whole 2x2x4 slice. The times are simulated.
32 devices in a mesh: row: 4 (over y, x), col: 8 (over z, core).
Axes of the slice: x: 2, y: 2, z: 4, core: 2. Of those that a mesh axis runs over, the one named last changes fastest.
Arguments:
- amplitudes: bfloat16 [4096, 262144], P(None, ('row', 'col')), may hold values from -6 to 6
- integrals: bfloat16 [64, 262144], P(None, ('row', 'col')), may hold values from -6 to 6
- hh_coupling: bfloat16 [64, 4096], P('row'), may hold values from -0.09375 to 0.09375
- thc_factor: bfloat16 [512, 1024], P(None, ('row', 'col')), may hold values from -0.25 to 0.25
- thc_core: float32 [1024, 1024], P('col', 'row'), may hold values from -3 to 3
- occ_energy: float32 [64], replicated, may hold values from -2 to -0.5
- vir_energy: float32 [512], replicated, may hold values from 0.3 to 3
- pair_owner: int32 [64], replicated, may hold values from 0 to 4095, as said below
Outputs:
- updated: bfloat16 [64, 262144], P(None, ('row', 'col'))
Inputs may be any that keep to these rules, and one draw needn't show every extreme that they name: pair_owner holds 64 distinct occupied pairs.
All inputs are finite; a program needn't handle non-finite values.
Results may differ from a plain program's by a relative error of at most 0.007.
Values may be sent and summed in bfloat16 or wider, within the bound.
No kernel may reach another device: no remote copies, remote signals or barrier semaphores. Data moves between devices by JAX's collectives and lax.ppermute only.
A program may use at most 128 MiB of HBM per device.

v0:
```python
import jax
import jax.numpy as jnp
from jax import lax
from jax.sharding import PartitionSpec as P


def per_device(
    amplitudes, integrals, hh_coupling, thc_factor, thc_core, occ_energy, vir_energy, pair_owner
):
    row_count = lax.axis_size("row")
    col_count = lax.axis_size("col")
    row_index = lax.axis_index("row")
    col_index = lax.axis_index("col")
    virtual = vir_energy.shape[0]
    column_width = amplitudes.shape[1]
    orb_block = column_width // virtual
    pairs_all = pair_owner.shape[0]
    pairs_col = pairs_all // col_count
    occupied = occ_energy.shape[0]
    factor = lax.all_gather(thc_factor, ("row", "col"), axis=1, tiled=True)
    points = factor.shape[1]
    block_points = points // row_count
    core_block = lax.all_gather(thc_core, "col", axis=0, tiled=True)
    factor_block = lax.dynamic_slice_in_dim(factor, row_index * block_points, block_points, 1)
    owned = amplitudes[pair_owner]
    coupled = jnp.dot(
        lax.all_gather(hh_coupling, "row", axis=0, tiled=True),
        amplitudes,
        preferred_element_type=jnp.float32,
    )
    outgoing = owned.reshape(col_count, pairs_col, column_width)
    arrived = lax.all_to_all(outgoing, "col", split_axis=0, concat_axis=2, tiled=True)
    complete = lax.all_gather(arrived, "row", axis=2, tiled=True)
    complete = complete.reshape(pairs_col, virtual, virtual)
    half = jnp.einsum(
        "pcd,dq->pcq", complete, factor_block, preferred_element_type=jnp.float32
    ).astype(jnp.bfloat16)
    middle = jnp.einsum("cP,pcq->pPq", factor, half, preferred_element_type=jnp.float32)
    weighted = (core_block[None] * middle).astype(jnp.bfloat16)
    back = jnp.einsum("aP,pPq->paq", factor, weighted, preferred_element_type=jnp.float32).astype(
        jnp.bfloat16
    )
    vir_slice = virtual // row_count
    sectioned_back = back.reshape(pairs_col, row_count, vir_slice, block_points)
    gathered_back = lax.all_to_all(sectioned_back, "row", split_axis=1, concat_axis=3, tiled=True)
    gathered_back = gathered_back.reshape(pairs_col, vir_slice, row_count, block_points)
    factor_split = factor.reshape(virtual, row_count, block_points)
    partial_value = jnp.einsum(
        "parq,brq->rapb", gathered_back, factor_split, preferred_element_type=jnp.float32
    ).astype(jnp.bfloat16)
    ladder = jnp.sum(partial_value.astype(jnp.float32), axis=0).astype(jnp.bfloat16)
    ladder = ladder.reshape(col_count, orb_block, pairs_col, virtual)
    returned = lax.all_to_all(ladder, "col", split_axis=0, concat_axis=2, tiled=True)
    returned = (
        returned.reshape(orb_block, pairs_all, virtual)
        .transpose(1, 0, 2)
        .reshape(pairs_all, column_width)
    )
    device = row_index * col_count + col_index
    vir_mine = lax.dynamic_slice_in_dim(vir_energy, device * orb_block, orb_block, 0)
    orbital_ids = jnp.arange(occupied, dtype=jnp.int32)
    first_hit = (pair_owner // occupied)[:, None] == orbital_ids[None, :]
    second_hit = (pair_owner % occupied)[:, None] == orbital_ids[None, :]
    first_occ = jnp.sum(jnp.where(first_hit, occ_energy[None, :], 0.0), axis=1)
    second_occ = jnp.sum(jnp.where(second_hit, occ_energy[None, :], 0.0), axis=1)
    vir_pairs = (vir_mine[:, None] + vir_energy[None, :]).reshape(1, column_width)
    denom = vir_pairs - (first_occ + second_occ)[:, None]
    rest = integrals.astype(jnp.float32) + coupled + returned.astype(jnp.float32)
    update = 0.4 * owned.astype(jnp.float32) + 0.6 * rest / denom
    return update.astype(jnp.bfloat16)


def solution(mesh):
    return jax.shard_map(
        per_device,
        mesh=mesh,
        in_specs=(
            P(None, ("row", "col")),
            P(None, ("row", "col")),
            P("row", None),
            P(None, ("row", "col")),
            P("col", "row"),
            P(),
            P(),
            P(),
        ),
        out_specs=P(None, ("row", "col")),
        check_vma=False,
    )
```

profile of v0, /device:TPU:0, one launch (start us, length us, event | category | flops | bytes accessed | tf_op | source)
XLA Modules:
  0.0 268.6 jit_solution(10117325499815692908)
XLA Ops:
  6.5 0.7 all-gather.4.cloned.1.call-update
  7.3 0.7 all-gather.8.cloned.1.call-update
  8.1 0.7 and_select_fusion.1
  8.7 3.7 %gather_fusion = bf16[64,8192]{1,0:T(8,128)(2,1)S(1)} fusion(bf16[4096,8192]{1,0:T(8,128)(2,1)} %param.8, s32[1024]{0:T(1024)S(1)} %pad_clamp_fusion), kind=kCustom, calls=%fused_computation | custom fusion | bytes 2097408 | tf_op jit(solution)/shard_map/gather | solution.py:25
  12.4 41.2 %all_to_all.45 = bf16[8,8,8192]{2,1,0:T(8,128)(2,1)} all-to-all(bf16[8,8,8192]{2,1,0:T(8,128)(2,1)S(1)} %bitcast.64), channel_id=1, replica_groups=mesh['row'=4,'col'=8] {'col'}, dimensions={0} | all-to-all | bytes 2097152 | tf_op jit(solution)/shard_map/all_to_all | solution.py:32
  53.7 1.6 copy.39
  55.3 44.9 %all-gather.8.cloned.1.call-done = bf16[512,1024]{0,1:T(8,128)(2,1)} async-done(((bf16[512,32]{0,1:T(8,128)(2,1)}), bf16[512,1024]{0,1:T(8,128)(2,1)}) %all-gather.8.cloned.1.call-update) | async-done | bytes 1048592 | tf_op jit(solution)/shard_map/all_gather | solution.py:20
  100.2 53.4 %all-gather.6.cloned.1.call-done = bf16[1,8,262144]{2,1,0:T(8,128)(2,1)} async-done(((bf16[1,8,65536]{2,1,0:T(8,128)(2,1)}), bf16[1,8,262144]{2,1,0:T(8,128)(2,1)}) %all-gather.6.cloned.1.call-update) | async-done | bytes 4194320 | tf_op jit(solution)/shard_map/all_gather | solution.py:33
  153.6 6.2 %fusion.8 = bf16[8,512,256]{2,1,0:T(8,128)(2,1)} fusion(bf16[1,8,512,512]{3,1,2,0:T(8,128)(2,1)} %bitcast.69, bf16[512,1024]{0,1:T(8,128)(2,1)} %all-gather.8.cloned.1.call-done, s32[]{:T(128)S(6)} %select_n.29), kind=kOutput, calls=%fused_computation.10 | convolution fusion | flops 1073741824 | bytes 6553604 | tf_op jit(solution)/shard_map/pcd,dq->pcq/dot_general | solution.py:35
  159.8 7.5 %convert_bitcast_fusion.1 = bf16[8,512,256]{1,2,0:T(8,128)(2,1)} fusion(f32[1024,256]{0,1:T(8,128)S(1)} %copy.39, bf16[8,512,256]{2,1,0:T(8,128)(2,1)} %fusion.8, bf16[512,1024]{0,1:T(8,128)(2,1)S(1)} %copy-done.3), kind=kOutput, calls=%fused_computation.18 | convolution fusion | flops 4300210176 | bytes 6291456 | tf_op jit(solution)/shard_map/aP,pPq->paq/dot_general | solution.py:40
  167.3 2.5 reshape.54
  169.9 2.5 copy.42
  172.4 29.2 %all_to_all.46 = bf16[8,4,128,256]{3,2,0,1:T(8,128)(2,1)S(1)} all-to-all(bf16[8,4,128,256]{3,2,0,1:T(8,128)(2,1)} %copy.42), channel_id=1, replica_groups=mesh['row'=4,'col'=8] {'row'}, dimensions={1} | all-to-all | bytes 4194304 | tf_op jit(solution)/shard_map/all_to_all | solution.py:45
  201.7 1.2 convert_reduce_fusion
  202.9 1.5 copy.44
  204.5 4.6 %all-to-all-start.2 = ((bf16[8,16,8,512]{3,2,1,0:T(8,128)(2,1)}), bf16[8,16,8,512]{3,2,1,0:T(8,128)(2,1)S(1)}, u32[]{:S(2)}, u32[]{:S(2)}) async-start(bf16[8,16,8,512]{3,2,1,0:T(8,128)(2,1)} %bitcast.14), calls=%async_computation.2 | async-start | bytes 2097152 | tf_op jit(solution)/shard_map/all_to_all | solution.py:53
  209.1 0.1 dynamic_slice.7
  209.2 0.1 add_bitcast_fusion
  209.3 0.2 select_reduce_fusion
  209.5 10.8 %all_gather.12 = bf16[64,4096]{1,0:T(8,128)(2,1)} all-gather(bf16[16,4096]{1,0:T(8,128)(2,1)S(1)} %copy-done), channel_id=1, replica_groups=mesh['row'=4,'col'=8] {'row'}, dimensions={0}, use_global_device_ids=true | all-gather | bytes 655360 | tf_op jit(solution)/shard_map/all_gather | solution.py:27
  220.3 15.3 %all-to-all-done.2 = bf16[8,16,8,512]{3,2,1,0:T(8,128)(2,1)S(1)} async-done(((bf16[8,16,8,512]{3,2,1,0:T(8,128)(2,1)}), bf16[8,16,8,512]{3,2,1,0:T(8,128)(2,1)S(1)}, u32[]{:S(2)}, u32[]{:S(2)}) %all-to-all-start.2) | async-done | bytes 1048608 | tf_op jit(solution)/shard_map/all_to_all | solution.py:53
  235.7 0.3 copy_bitcast_fusion
  235.9 0.2 copy.52
  236.2 25.9 %fusion.4 = bf16[64,8192]{1,0:T(8,128)(2,1)} fusion(f32[64,8192]{1,0:T(8,128)S(1)} %bitcast.65, bf16[64,4096]{1,0:T(8,128)(2,1)} %all_gather.12, bf16[4096,8192]{1,0:T(8,128)(2,1)} %param.8, bf16[64,8192]{1,0:T(8,128)(2,1)} %param.9, bf16[64,8192]{1,0:T(8,128)(2,1)S(1)} %gather_fusion, f32[64]{0:T(128)S(1)} %add.70, f32[8192]{0:T(1024)S(1)} %bitcast.68), kind=kOutput, calls=%fused_computation.6 | convolution fusion | flops 4300210176 | bytes 72909056 | tf_op jit(solution)/shard_map/dot_general | solution.py:26
  (18 shorter events, 0.2 us)
Async XLA Ops:
  6.5 47.2 %all-gather.4.cloned.1.call-start = ((), (), s32[]{:S(2)}) async-start(), calls=%async_computation.3 | async-start | bytes 1179648 | tf_op jit(solution)/shard_map/all_gather | solution.py:23
  7.3 92.9 %all-gather.8.cloned.1.call-start = ((), (), s32[]{:S(2)}) async-start(), calls=%async_computation.5 | async-start | bytes 1081344 | tf_op jit(solution)/shard_map/all_gather | solution.py:20
  8.0 145.6 %all-gather.6.cloned.1.call-start = ((), (), s32[]{:S(2)}) async-start(), calls=%async_computation.4 | async-start | bytes 5242880 | tf_op jit(solution)/shard_map/all_gather | solution.py:33
  153.6 6.2 %copy-start.3 = (bf16[512,1024]{0,1:T(8,128)(2,1)S(1)}, bf16[512,1024]{0,1:T(8,128)(2,1)}, u32[]{:S(2)}) copy-start(bf16[512,1024]{0,1:T(8,128)(2,1)} %all-gather.8.cloned.1.call-done) | copy-start | bytes 3145732
  172.4 29.2 %copy-start.4 = (bf16[512,1024]{0,1:T(8,128)(2,1)S(1)}, bf16[512,1024]{0,1:T(8,128)(2,1)}, u32[]{:S(2)}) copy-start(bf16[512,1024]{0,1:T(8,128)(2,1)} %all-gather.8.cloned.1.call-done) | copy-start | bytes 3145732
  202.9 6.2 %copy-start.1 = (f32[512]{0:T(512)S(1)}, f32[512]{0:T(512)}, u32[]{:S(2)}) copy-start(f32[512]{0:T(512)} %param.14) | copy-start | bytes 6148
  202.9 6.4 %copy-start.2 = (f32[64]{0:T(128)S(1)}, f32[64]{0:T(128)}, u32[]{:S(2)}) copy-start(f32[64]{0:T(128)} %param.13) | copy-start | bytes 772
  202.9 6.5 %copy-start = (bf16[16,4096]{1,0:T(8,128)(2,1)S(1)}, bf16[16,4096]{1,0:T(8,128)(2,1)}, u32[]{:S(2)}) copy-start(bf16[16,4096]{1,0:T(8,128)(2,1)} %param.10) | copy-start | bytes 393220
  204.5 31.2 %all-to-all-start.2 = ((bf16[8,16,8,512]{3,2,1,0:T(8,128)(2,1)}), bf16[8,16,8,512]{3,2,1,0:T(8,128)(2,1)S(1)}, u32[]{:S(2)}, u32[]{:S(2)}) async-start(bf16[8,16,8,512]{3,2,1,0:T(8,128)(2,1)} %bitcast.14), calls=%async_computation.2 | async-start | bytes 2097152 | tf_op jit(solution)/shard_map/all_to_all | solution.py:53
Sparse Core Ops, SparseCore 0:
  8.9 34.5 all-gather.3
  46.5 53.6 all-gather.7
  102.0 51.5 all-gather.5
where the time goes:
time: 269 us
  waiting for transfers between devices  115 us (43%)
  blocking collectives  81.3 us (30%)
  matrix products  40.8 us (15%)
  between operations  13.2 us (5%)
  local copies, waits for them, and re-layouts  12.2 us (5%)
  starting transfers between devices  4.69 us (2%)
    all_gather x1, waiting for transfers between devices, per_device(): complete = lax.all_gather(arrived, 'row', axis=2, tiled=True)  53.4 us
    all_gather x1, waiting for transfers between devices, per_device(): factor = lax.all_gather(thc_factor, ('row', 'col'), axis=1, tiled=True)  44.9 us
    all_to_all x1, blocking collectives, per_device(): lax.all_to_all(outgoing, 'col', split_axis=0, concat_axis=2, tiled=True)  41.2 us
    all_to_all x1, blocking collectives, per_device(): lax.all_to_all(sectioned_back, 'row', split_axis=1, concat_axis=3, tiled=...  29.2 us
    dot_general x1, matrix products, per_device(): jnp.dot(lax.all_gather(hh_coupling, 'row', axis=0, tiled=True), amplitude...  25.9 us
    all_to_all x1, waiting for transfers between devices, per_device(): lax.all_to_all(ladder, 'col', split_axis=0, concat_axis=2, tiled=True)  15.3 us
    all_gather x1, blocking collectives, per_device(): lax.all_gather(hh_coupling, 'row', axis=0, tiled=True)  10.8 us
    dot_general x1, matrix products, per_device(): jnp.einsum('aP,pPq->paq', factor, weighted, preferred_element_type=jnp.fl...  7.51 us
  transfers between devices with their start and end apart: 4, of which 3 were waited for; matrix products, arithmetic and copies ran while one was open for 2% of the time, Pallas kernels for 0%

commit v1 on v0

v1 whole, which is shorter than its diff:
```python
import functools
import jax
import jax.numpy as jnp
from jax import lax
from jax.experimental import pallas as pl
from jax.experimental.pallas import tpu as pltpu
from jax.sharding import PartitionSpec as P

F32, BF16 = jnp.float32, jnp.bfloat16
AXES = ("row", "col")


def dot(a, b, ca, cb):
    return lax.dot_general(a, b, (((ca,), (cb,)), ((), ())), preferred_element_type=F32)


def exchange(value, flip_row, flip_col):
    rows, cols = lax.axis_size("row"), lax.axis_size("col")
    pairs = [
        (r * cols + c, (r ^ flip_row) * cols + (c ^ flip_col))
        for r in range(rows)
        for c in range(cols)
    ]
    return lax.ppermute(value, AXES, pairs)


def owner_terms(pair_owner, occ_energy):
    occupied = occ_energy.shape[0]
    orbital_ids = jnp.arange(occupied, dtype=jnp.int32)
    first_hit = (pair_owner // occupied)[:, None] == orbital_ids[None, :]
    second_hit = (pair_owner % occupied)[:, None] == orbital_ids[None, :]
    first_occ = jnp.sum(jnp.where(first_hit, occ_energy[None, :], 0.0), axis=1)
    second_occ = jnp.sum(jnp.where(second_hit, occ_energy[None, :], 0.0), axis=1)
    return first_occ + second_occ


def place_kernel(spec, *refs):
    parts, points, virtual = spec
    n_in = len(parts)
    ins, (xt_ref, x_ref, core_ref) = refs[:n_in], refs[n_in:]
    row, col = lax.axis_index("row"), lax.axis_index("col")
    wide = virtual // 2
    for ref, entries in zip(ins, parts):
        for slot, (flip_row, flip_col) in enumerate(entries):
            r, c = row ^ flip_row, col ^ flip_col
            cols = lax.axis_size("col")
            j = r * cols + c
            fine = points // (lax.axis_size("row") * cols)
            deep = points // cols
            at = pl.multiple_of(j * fine, fine)
            xt_ref[pl.ds(at, fine), :wide] = ref[slot, :fine, :]
            xt_ref[pl.ds(at, fine), wide:] = ref[slot, fine : 2 * fine, :]
            core_ref[r, pl.ds(pl.multiple_of(c * deep, deep), deep), :] = ref[slot, 2 * fine :, :]
    x_ref[...] = xt_ref[...].T


def ladder_kernel(a_ref, xt_ref, x_ref, core_ref, out_ref, acc_ref):
    blocks, points, block = core_ref.shape
    virtual = xt_ref.shape[1]
    a = a_ref[...].reshape(virtual, virtual)
    for r in range(blocks):
        xq = xt_ref[r * block : (r + 1) * block, :]
        half = dot(a, xq, 1, 1).astype(BF16)
        middle = dot(xt_ref[...], half, 1, 0)
        weighted = (core_ref[r].astype(F32) * middle).astype(BF16)
        back = dot(x_ref[...], weighted, 1, 0).astype(BF16)
        term = dot(back, xq, 1, 0)
        if r == 0:
            acc_ref[...] = term
        else:
            acc_ref[...] += term
    out_ref[...] = acc_ref[...].astype(BF16).reshape(out_ref.shape)


def whole_pairs(
    amplitudes, integrals, hh_coupling, thc_factor, thc_core, occ_energy, vir_energy, pair_owner
):
    row_count, col_count = lax.axis_size("row"), lax.axis_size("col")
    row, col = lax.axis_index("row"), lax.axis_index("col")
    devices = row_count * col_count
    virtual = vir_energy.shape[0]
    width = amplitudes.shape[1]
    orbs = width // virtual
    pairs_all = pair_owner.shape[0]
    mine = pairs_all // devices
    occupied_pairs = amplitudes.shape[0]
    points = thc_factor.shape[1] * devices
    block = points // row_count

    xt = thc_factor.T
    own = jnp.concatenate([xt[:, : virtual // 2], xt[:, virtual // 2 :], thc_core.astype(BF16)], 0)

    with jax.named_scope("hh_gather"):
        hh_parts = [hh_coupling] + [exchange(hh_coupling, t, 0) for t in range(1, row_count)]
    hh_rows = hh_coupling.shape[0]
    hh_all = jnp.zeros((hh_rows * row_count, occupied_pairs), BF16)
    for t, part in enumerate(hh_parts):
        hh_all = lax.dynamic_update_slice_in_dim(hh_all, part, (row ^ t) * hh_rows, 0)

    with jax.named_scope("z_gather"):
        z_flips = list(range(0, col_count, 2))
        stack = jnp.stack([own] + [exchange(own, 0, f) for f in z_flips[1:]])
    near = {0: stack}
    with jax.named_scope("xy_gather"):
        near[1] = exchange(stack, 1, 0)
        near[2] = exchange(stack, 2, 0)
        cut = len(z_flips) // 2
        low = exchange(near[1][:cut], 2, 0)
        high = exchange(near[2][cut:], 1, 0)
    arrays, places = [], []
    for t in (0, 1, 2):
        arrays.append(near[t])
        places.append([(t, f) for f in z_flips])
    arrays += [low, high]
    places += [[(3, f) for f in z_flips[:cut]], [(3, f) for f in z_flips[cut:]]]
    with jax.named_scope("core_gather"):
        for array, place in list(zip(arrays, places)):
            arrays.append(exchange(array, 0, 1))
            places.append([(r, f ^ 1) for r, f in place])

    owned = amplitudes[pair_owner]
    with jax.named_scope("pair_out"):
        outgoing = owned.reshape(devices, mine, orbs, virtual)
        arrived = lax.all_to_all(outgoing, AXES, split_axis=0, concat_axis=0, tiled=True)

    with jax.named_scope("coupled"):
        coupled = jnp.dot(hh_all, amplitudes, preferred_element_type=F32)

    xt_full, x_full, core_full = pl.pallas_call(
        functools.partial(place_kernel, (places, points, virtual)),
        out_shape=[
            jax.ShapeDtypeStruct((points, virtual), BF16),
            jax.ShapeDtypeStruct((virtual, points), BF16),
            jax.ShapeDtypeStruct((row_count, points, block), BF16),
        ],
        cost_estimate=pl.CostEstimate(flops=0, bytes_accessed=8 << 20, transcendentals=0),
        name="place",
    )(*arrays)

    ladder = pl.pallas_call(
        ladder_kernel,
        grid=(mine,),
        in_specs=[
            pl.BlockSpec((devices, pl.squeezed, orbs, virtual), lambda p: (0, p, 0, 0)),
            pl.BlockSpec((points, virtual), lambda p: (0, 0)),
            pl.BlockSpec((virtual, points), lambda p: (0, 0)),
            pl.BlockSpec((row_count, points, block), lambda p: (0, 0, 0)),
        ],
        out_specs=pl.BlockSpec((devices, pl.squeezed, orbs, virtual), lambda p: (0, p, 0, 0)),
        out_shape=jax.ShapeDtypeStruct((devices, mine, orbs, virtual), BF16),
        scratch_shapes=[pltpu.VMEM((virtual, virtual), F32)],
        cost_estimate=pl.CostEstimate(
            flops=mine * 2 * virtual * points * (2 * virtual + 2 * points),
            bytes_accessed=6 << 20,
            transcendentals=0,
        ),
        name="ladder",
    )(arrived, xt_full, x_full, core_full)

    with jax.named_scope("pair_back"):
        returned = lax.all_to_all(ladder, AXES, split_axis=0, concat_axis=0, tiled=True)
        returned = returned.reshape(pairs_all, width)

    coupled = lax.optimization_barrier(coupled)
    device = row * col_count + col
    vir_mine = lax.dynamic_slice_in_dim(vir_energy, device * orbs, orbs, 0)
    occ = owner_terms(pair_owner, occ_energy)
    vir_pairs = (vir_mine[:, None] + vir_energy[None, :]).reshape(1, width)
    denom = vir_pairs - occ[:, None]
    rest = integrals.astype(F32) + coupled + returned.astype(F32)
    update = 0.4 * owned.astype(F32) + 0.6 * rest / denom
    return update.astype(BF16)


def shared_pairs(
    amplitudes, integrals, hh_coupling, thc_factor, thc_core, occ_energy, vir_energy, pair_owner
):
    row_count, col_count = lax.axis_size("row"), lax.axis_size("col")
    row_index, col_index = lax.axis_index("row"), lax.axis_index("col")
    virtual = vir_energy.shape[0]
    column_width = amplitudes.shape[1]
    orb_block = column_width // virtual
    pairs_all = pair_owner.shape[0]
    pairs_col = pairs_all // col_count
    factor = lax.all_gather(thc_factor, AXES, axis=1, tiled=True)
    points = factor.shape[1]
    block_points = points // row_count
    core_block = lax.all_gather(thc_core, "col", axis=0, tiled=True)
    factor_block = lax.dynamic_slice_in_dim(factor, row_index * block_points, block_points, 1)
    owned = amplitudes[pair_owner]
    coupled = jnp.dot(
        lax.all_gather(hh_coupling, "row", axis=0, tiled=True),
        amplitudes,
        preferred_element_type=F32,
    )
    outgoing = owned.reshape(col_count, pairs_col, column_width)
    arrived = lax.all_to_all(outgoing, "col", split_axis=0, concat_axis=2, tiled=True)
    complete = lax.all_gather(arrived, "row", axis=2, tiled=True)
    complete = complete.reshape(pairs_col, virtual, virtual)
    half = jnp.einsum("pcd,dq->pcq", complete, factor_block, preferred_element_type=F32)
    half = half.astype(BF16)
    middle = jnp.einsum("cP,pcq->pPq", factor, half, preferred_element_type=F32)
    weighted = (core_block[None] * middle).astype(BF16)
    back = jnp.einsum("aP,pPq->paq", factor, weighted, preferred_element_type=F32).astype(BF16)
    vir_slice = virtual // row_count
    sectioned_back = back.reshape(pairs_col, row_count, vir_slice, block_points)
    gathered_back = lax.all_to_all(sectioned_back, "row", split_axis=1, concat_axis=3, tiled=True)
    gathered_back = gathered_back.reshape(pairs_col, vir_slice, row_count, block_points)
    factor_split = factor.reshape(virtual, row_count, block_points)
    partial_value = jnp.einsum(
        "parq,brq->rapb", gathered_back, factor_split, preferred_element_type=F32
    ).astype(BF16)
    ladder = jnp.sum(partial_value.astype(F32), axis=0).astype(BF16)
    ladder = ladder.reshape(col_count, orb_block, pairs_col, virtual)
    returned = lax.all_to_all(ladder, "col", split_axis=0, concat_axis=2, tiled=True)
    returned = (
        returned.reshape(orb_block, pairs_all, virtual)
        .transpose(1, 0, 2)
        .reshape(pairs_all, column_width)
    )
    device = row_index * col_count + col_index
    vir_mine = lax.dynamic_slice_in_dim(vir_energy, device * orb_block, orb_block, 0)
    occ = owner_terms(pair_owner, occ_energy)
    vir_pairs = (vir_mine[:, None] + vir_energy[None, :]).reshape(1, column_width)
    denom = vir_pairs - occ[:, None]
    rest = integrals.astype(F32) + coupled + returned.astype(F32)
    update = 0.4 * owned.astype(F32) + 0.6 * rest / denom
    return update.astype(BF16)


def per_device(*arguments):
    rows, cols = lax.axis_size("row"), lax.axis_size("col")
    pairs_all = arguments[-1].shape[0]
    if rows == 4 and cols & (cols - 1) == 0 and pairs_all % (rows * cols) == 0:
        return whole_pairs(*arguments)
    return shared_pairs(*arguments)


def solution(mesh):
    return jax.shard_map(
        per_device,
        mesh=mesh,
        in_specs=(
            P(None, ("row", "col")),
            P(None, ("row", "col")),
            P("row", None),
            P(None, ("row", "col")),
            P("col", "row"),
            P(),
            P(),
            P(),
        ),
        out_specs=P(None, ("row", "col")),
        check_vma=False,
    )
```

time: 269 us -> 111 us (0.41)
  waiting for transfers between devices: 115 us -> 28.1 us
  blocking collectives: 81.3 us -> 0 us
  starting transfers between devices: 4.69 us -> 24.4 us
  matrix products: 40.8 us -> 23.6 us
  Pallas kernels: 0 us -> 17.1 us
  between operations: 13.2 us -> 0.29 us
    all_gather x3 -> x0, waiting for transfers between devices: 98.4 us -> none  [the longest x1 53.4 us: per_device(): complete = lax.all_gather(arrived, 'row', axis=2, tiled=True)]
    all_to_all x2 -> x0, blocking collectives: 70.4 us -> none  [the longest x1 41.2 us: per_device(): lax.all_to_all(outgoing, 'col', split_axis=0, concat_axis=2, tiled=True)]
    ppermute x0 -> x15, waiting for transfers between devices: none -> 24.4 us  [exchange(): return lax.ppermute(value, AXES, pairs)]
    dot_general x4 -> x1, matrix products: 40.8 us -> 23.6 us  [whole_pairs(): coupled = jnp.dot(hh_all, amplitudes, preferred_element_type=F32)]
    pallas_call x0 -> x2, Pallas kernels: none -> 17.1 us  [the longest x1 13 us: whole_pairs(): pl.pallas_call(ladder_kernel, grid=(mine,), in_specs=[pl.BlockSpec((devic...]
    ppermute x0 -> x15, starting transfers between devices: none -> 15.1 us  [exchange(): return lax.ppermute(value, AXES, pairs)]
    all_to_all x1 -> x2, waiting for transfers between devices: 15.3 us -> 3.68 us  [the longest x1 3.67 us: whole_pairs(): lax.all_to_all(ladder, AXES, split_axis=0, concat_axis=0, tiled=True)]
    all_gather x1 -> x0, blocking collectives: 10.8 us -> none  [per_device(): lax.all_gather(hh_coupling, 'row', axis=0, tiled=True)]
  transfers between devices with their start and end apart: 4 -> 17, of which waited for: 3 -> 6; matrix products, arithmetic and copies ran while one was open for 2% -> 29% of each run, Pallas kernels for 0% -> 4%
where the time goes in v1:
time: 111 us; the launch traced here: 110 us
  waiting for transfers between devices  28.1 us (25%)
  starting transfers between devices  24.4 us (22%)
  matrix products  23.6 us (21%)
  Pallas kernels  17.1 us (15%)
  local copies, waits for them, and re-layouts  12.9 us (12%)
  other arithmetic  3.61 us (3%)
    ppermute x15, waiting for transfers between devices, exchange(): return lax.ppermute(value, AXES, pairs)  24.4 us
    dot_general x1, matrix products, whole_pairs(): coupled = jnp.dot(hh_all, amplitudes, preferred_element_type=F32)  23.6 us
    ppermute x15, starting transfers between devices, exchange(): return lax.ppermute(value, AXES, pairs)  15.1 us
    pallas_call x1, Pallas kernels, whole_pairs(): pl.pallas_call(ladder_kernel, grid=(mine,), in_specs=[pl.BlockSpec((devic...  13 us
    unnamed x31, local copies, waits for them, and re-layouts  5.69 us
    all_to_all x1, starting transfers between devices, whole_pairs(): lax.all_to_all(ladder, AXES, split_axis=0, concat_axis=0, tiled=True)  5.34 us
    pallas_call x1, Pallas kernels, whole_pairs(): pl.pallas_call(functools.partial(place_kernel, (places, points, virtual))...  4.09 us
    all_to_all x1, starting transfers between devices, whole_pairs(): lax.all_to_all(outgoing, AXES, split_axis=0, concat_axis=0, tiled=True)  3.97 us
  transfers between devices with their start and end apart: 17, of which 6 were waited for; matrix products, arithmetic and copies ran while one was open for 29% of the time, Pallas kernels for 4%

profile of v1, /device:TPU:0, one launch (start us, length us, event | category | flops | bytes accessed | tf_op | source)
XLA Modules:
  0.0 110.0 jit_solution(386929396020775278)
XLA Ops:
  1.7 3.1 %collective-permute-start.3 = (bf16[192,256]{1,0:T(8,128)(2,1)S(1)}, bf16[192,256]{1,0:T(8,128)(2,1)S(1)}, u32[]{:S(2)}, u32[]{:S(2)}) collective-permute-start(bf16[192,256]{1,0:T(8,128)(2,1)S(1)} %get-tuple-element.14), channel_id=1, source_target_pairs={{0,2},{1,3},{2,0},{3,1},{4,6},{5,7},{6,4},{7,5},{8,10},{9,11},{10,... | collective-permute-start | bytes 294920 | tf_op jit(solution)/shard_map/z_gather/ppermute | solution.py:24
  4.8 2.6 %collective-permute-start.4 = (bf16[192,256]{1,0:T(8,128)(2,1)S(1)}, bf16[192,256]{1,0:T(8,128)(2,1)S(1)}, u32[]{:S(2)}, u32[]{:S(2)}) collective-permute-start(bf16[192,256]{1,0:T(8,128)(2,1)S(1)} %get-tuple-element.14), channel_id=1, source_target_pairs={{0,4},{1,5},{2,6},{3,7},{4,0},{5,1},{6,2},{7,3},{8,12},{9,13},{10,... | collective-permute-start | bytes 294920 | tf_op jit(solution)/shard_map/z_gather/ppermute | solution.py:24
  7.4 1.7 %collective-permute-start = (bf16[16,4096]{1,0:T(8,128)(2,1)}, bf16[16,4096]{1,0:T(8,128)(2,1)}, u32[]{:S(2)}, u32[]{:S(2)}) collective-permute-start(bf16[16,4096]{1,0:T(8,128)(2,1)} %param.10), channel_id=1, source_target_pairs={{0,8},{1,9},{2,10},{3,11},{4,12},{5,13},{6,14},{7,15},{8,0},{9,1},... | collective-permute-start | bytes 393224 | tf_op jit(solution)/shard_map/hh_gather/ppermute | solution.py:24
  9.1 1.5 %collective-permute-start.1 = (bf16[16,4096]{1,0:T(8,128)(2,1)}, bf16[16,4096]{1,0:T(8,128)(2,1)}, u32[]{:S(2)}, u32[]{:S(2)}) collective-permute-start(bf16[16,4096]{1,0:T(8,128)(2,1)} %param.10), channel_id=1, source_target_pairs={{0,16},{1,17},{2,18},{3,19},{4,20},{5,21},{6,22},{7,23},{8,24},{9,... | collective-permute-start | bytes 393224 | tf_op jit(solution)/shard_map/hh_gather/ppermute | solution.py:24
  11.3 3.6 %gather_fusion = bf16[64,8192]{1,0:T(8,128)(2,1)S(1)} fusion(bf16[4096,8192]{1,0:T(8,128)(2,1)} %param.8, s32[1024]{0:T(1024)S(1)} %pad_clamp_fusion), kind=kCustom, calls=%fused_computation | custom fusion | bytes 2097408 | tf_op jit(solution)/shard_map/gather | solution.py:121
  14.9 1.3 %copy.9 = bf16[8,8,16,512]{3,2,1,0:T(8,128)(2,1)} copy(bf16[8,8,16,512]{3,1,2,0:T(8,128)(2,1)S(1)} %bitcast.18) | data formatting | bytes 2097152
  16.2 4.0 %all-to-all-start = ((bf16[32,2,16,512]{3,2,1,0:T(8,128)(2,1)}), bf16[32,2,16,512]{3,2,1,0:T(8,128)(2,1)S(1)}, u32[]{:S(2)}, u32[]{:S(2)}) async-start(bf16[32,2,16,512]{3,2,1,0:T(8,128)(2,1)} %bitcast.7), calls=%async_computation | async-start | bytes 2097152 | tf_op jit(solution)/shard_map/pair_out/all_to_all | solution.py:124
  20.4 0.9 constant_dynamic-update-slice_fusion.3
  21.6 2.7 %collective-permute-start.2 = (bf16[16,4096]{1,0:T(8,128)(2,1)}, bf16[16,4096]{1,0:T(8,128)(2,1)S(1)}, u32[]{:S(2)}, u32[]{:S(2)}) collective-permute-start(bf16[16,4096]{1,0:T(8,128)(2,1)} %param.10), channel_id=1, source_target_pairs={{0,24},{1,25},{2,26},{3,27},{4,28},{5,29},{6,30},{7,31},{8,16},{9,... | collective-permute-start | bytes 393224 | tf_op jit(solution)/shard_map/hh_gather/ppermute | solution.py:24
  25.3 0.9 constant_dynamic-update-slice_fusion.2
  26.2 18.8 %collective-permute-done.6.refs_1_ = bf16[4,192,256]{2,1,0:T(8,128)(2,1)S(1)} collective-permute-done((bf16[4,192,256]{2,1,0:T(8,128)(2,1)S(1)}, bf16[4,192,256]{2,1,0:T(8,128)(2,1)S(1)}, u32[]{:S(2)}, u32[]{:S(2)}) %collective-permute-start.6) | collective-permute-done | bytes 393248 | tf_op jit(solution)/shard_map/xy_gather/ppermute | solution.py:24
  45.0 1.5 %collective-permute-start.8 = (bf16[2,192,256]{2,1,0:T(8,128)(2,1)S(1)}, bf16[2,192,256]{2,1,0:T(8,128)(2,1)S(1)}, u32[]{:S(2)}, u32[]{:S(2)}) collective-permute-start(bf16[2,192,256]{2,1,0:T(8,128)(2,1)S(1)} %slice.20), channel_id=1, source_target_pairs={{0,16},{1,17},{2,18},{3,19},{4,20},{5,21},{6,22},{7,23},{8,24},{9,... | collective-permute-start | bytes 589832 | tf_op jit(solution)/shard_map/xy_gather/ppermute | solution.py:24
  47.0 0.9 constant_dynamic-update-slice_fusion.1
  48.5 3.2 %collective-permute-done.8.refs_3_ = bf16[2,192,256]{2,1,0:T(8,128)(2,1)S(1)} collective-permute-done((bf16[2,192,256]{2,1,0:T(8,128)(2,1)S(1)}, bf16[2,192,256]{2,1,0:T(8,128)(2,1)S(1)}, u32[]{:S(2)}, u32[]{:S(2)}) %collective-permute-start.8) | collective-permute-done | bytes 196640 | tf_op jit(solution)/shard_map/xy_gather/ppermute | solution.py:24
  51.7 1.0 collective-permute-done.9.refs_4_
  53.1 1.0 collective-permute-done.14.refs_9_
  55.6 4.1 %place.1 = (bf16[1024,512]{1,0:T(8,128)(2,1)}, bf16[512,1024]{1,0:T(8,128)(2,1)}, bf16[4,1024,256]{2,1,0:T(8,128)(2,1)}) custom-call(bf16[4,192,256]{2,1,0:T(8,128)(2,1)} %copy-done.1, bf16[4,192,256]{2,1,0:T(8,128)(2,1)} %copy-done.4, bf16[4,192,256]{2,1,0:T(8,128)(2,1)} %copy-done.5, bf16[2,192,256]{2,1,0:T(8,128)(2,1)} %copy-done.8, ...), custom_call_target="tpu_custom_call" | custom-call | bytes 8388608 | tf_op jit(solution)/shard_map/place/pallas_call | solution.py:129
  59.7 1.0 copy-done.2
  60.7 13.0 %ladder.1 = bf16[32,2,16,512]{3,2,1,0:T(8,128)(2,1)} custom-call(bf16[32,2,16,512]{3,2,1,0:T(8,128)(2,1)} %copy-done.2, bf16[1024,512]{1,0:T(8,128)(2,1)} %get-tuple-element.8.xt_ref, bf16[512,1024]{1,0:T(8,128)(2,1)} %get-tuple-element.9.x_ref, bf16[4,1024,256]{2,1,0:T(8,128)(2,1)} %get-tuple-element.10.core_ref), custom_call_target="tpu_custom_call" | custom-call | flops 6442450944 | bytes 6291456 | tf_op jit(solution)/shard_map/ladder/pallas_call | solution.py:140
  73.7 5.3 %all-to-all-start.1 = ((bf16[32,2,16,512]{3,2,1,0:T(8,128)(2,1)}), bf16[32,2,16,512]{3,2,1,0:T(8,128)(2,1)}, u32[]{:S(2)}, u32[]{:S(2)}) async-start(bf16[32,2,16,512]{3,2,1,0:T(8,128)(2,1)} %ladder.1), calls=%async_computation.1 | async-start | bytes 2097152 | tf_op jit(solution)/shard_map/pair_back/all_to_all | solution.py:161
  79.1 23.6 %fusion.2 = f32[64,8192]{1,0:T(8,128)S(1)} fusion(bf16[64,4096]{1,0:T(8,128)(2,1)} %copy-done, bf16[4096,8192]{1,0:T(8,128)(2,1)} %param.8), kind=kOutput, calls=%fused_computation.22 | convolution fusion | flops 4294967296 | bytes 69730304 | tf_op jit(solution)/shard_map/coupled/dot_general | solution.py:127
  102.7 3.7 %all-to-all-done.1 = bf16[32,2,16,512]{3,2,1,0:T(8,128)(2,1)} async-done(((bf16[32,2,16,512]{3,2,1,0:T(8,128)(2,1)}), bf16[32,2,16,512]{3,2,1,0:T(8,128)(2,1)}, u32[]{:S(2)}, u32[]{:S(2)}) %all-to-all-start.1) | async-done | bytes 1048608 | tf_op jit(solution)/shard_map/pair_back/all_to_all | solution.py:161
  106.3 1.9 %copy.10 = f32[8,8,16,512]{3,1,2,0:T(8,128)S(1)} copy(bf16[8,8,16,512]{3,2,1,0:T(8,128)(2,1)} %bitcast.15) | data formatting | bytes 3145728
  108.3 1.7 %add_convert_fusion = bf16[64,8192]{1,0:T(8,128)(2,1)} fusion(f32[64,8192]{1,0:T(8,128)S(1)} %bitcast.19, f32[64,8192]{1,0:T(8,128)S(1)} %fusion.2, bf16[64,8192]{1,0:T(8,128)(2,1)S(1)} %copy-done.3, bf16[64,8192]{1,0:T(8,128)(2,1)S(1)} %gather_fusion, f32[64]{0:T(128)S(1)} %add.82, f32[8192]{0:T(1024)S(1)} %bitcast.20), kind=kLoop, calls=%fused_computation.1 | loop fusion | flops 5242880 | bytes 7373056 | tf_op jit(solution)/shard_map/convert_element_type | solution.py:172
  (63 shorter events, 6.5 us)
Async XLA Ops:
  1.7 19.9 %collective-permute-start.3 = (bf16[192,256]{1,0:T(8,128)(2,1)S(1)}, bf16[192,256]{1,0:T(8,128)(2,1)S(1)}, u32[]{:S(2)}, u32[]{:S(2)}) collective-permute-start(bf16[192,256]{1,0:T(8,128)(2,1)S(1)} %get-tuple-element.14), channel_id=1, source_target_pairs={{0,2},{1,3},{2,0},{3,1},{4,6},{5,7},{6,4},{7,5},{8,10},{9,11},{10,... | collective-permute-start | bytes 294920 | tf_op jit(solution)/shard_map/z_gather/ppermute | solution.py:24
  4.8 19.6 %collective-permute-start.4 = (bf16[192,256]{1,0:T(8,128)(2,1)S(1)}, bf16[192,256]{1,0:T(8,128)(2,1)S(1)}, u32[]{:S(2)}, u32[]{:S(2)}) collective-permute-start(bf16[192,256]{1,0:T(8,128)(2,1)S(1)} %get-tuple-element.14), channel_id=1, source_target_pairs={{0,4},{1,5},{2,6},{3,7},{4,0},{5,1},{6,2},{7,3},{8,12},{9,13},{10,... | collective-permute-start | bytes 294920 | tf_op jit(solution)/shard_map/z_gather/ppermute | solution.py:24
  7.4 17.0 %collective-permute-start.5 = (bf16[192,256]{1,0:T(8,128)(2,1)S(1)}, bf16[192,256]{1,0:T(8,128)(2,1)S(1)}, u32[]{:S(2)}, u32[]{:S(2)}) collective-permute-start(bf16[192,256]{1,0:T(8,128)(2,1)S(1)} %get-tuple-element.14), channel_id=1, source_target_pairs={{0,6},{1,7},{2,4},{3,5},{4,2},{5,3},{6,0},{7,1},{8,14},{9,15},{10,... | collective-permute-start | bytes 294920 | tf_op jit(solution)/shard_map/z_gather/ppermute | solution.py:24
  7.4 17.9 %collective-permute-start = (bf16[16,4096]{1,0:T(8,128)(2,1)}, bf16[16,4096]{1,0:T(8,128)(2,1)}, u32[]{:S(2)}, u32[]{:S(2)}) collective-permute-start(bf16[16,4096]{1,0:T(8,128)(2,1)} %param.10), channel_id=1, source_target_pairs={{0,8},{1,9},{2,10},{3,11},{4,12},{5,13},{6,14},{7,15},{8,0},{9,1},... | collective-permute-start | bytes 393224 | tf_op jit(solution)/shard_map/hh_gather/ppermute | solution.py:24
  9.1 37.9 %collective-permute-start.1 = (bf16[16,4096]{1,0:T(8,128)(2,1)}, bf16[16,4096]{1,0:T(8,128)(2,1)}, u32[]{:S(2)}, u32[]{:S(2)}) collective-permute-start(bf16[16,4096]{1,0:T(8,128)(2,1)} %param.10), channel_id=1, source_target_pairs={{0,16},{1,17},{2,18},{3,19},{4,20},{5,21},{6,22},{7,23},{8,24},{9,... | collective-permute-start | bytes 393224 | tf_op jit(solution)/shard_map/hh_gather/ppermute | solution.py:24
  14.9 5.3 %copy-start.12 = (f32[512]{0:T(512)S(1)}, f32[512]{0:T(512)}, u32[]{:S(2)}) copy-start(f32[512]{0:T(512)} %param.14) | copy-start | bytes 6148
  14.9 6.4 %copy-start.13 = (f32[64]{0:T(128)S(1)}, f32[64]{0:T(128)}, u32[]{:S(2)}) copy-start(f32[64]{0:T(128)} %param.13) | copy-start | bytes 772
  16.2 43.5 %all-to-all-start = ((bf16[32,2,16,512]{3,2,1,0:T(8,128)(2,1)}), bf16[32,2,16,512]{3,2,1,0:T(8,128)(2,1)S(1)}, u32[]{:S(2)}, u32[]{:S(2)}) async-start(bf16[32,2,16,512]{3,2,1,0:T(8,128)(2,1)} %bitcast.7), calls=%async_computation | async-start | bytes 2097152 | tf_op jit(solution)/shard_map/pair_out/all_to_all | solution.py:124
  21.6 26.4 %collective-permute-start.2 = (bf16[16,4096]{1,0:T(8,128)(2,1)}, bf16[16,4096]{1,0:T(8,128)(2,1)S(1)}, u32[]{:S(2)}, u32[]{:S(2)}) collective-permute-start(bf16[16,4096]{1,0:T(8,128)(2,1)} %param.10), channel_id=1, source_target_pairs={{0,24},{1,25},{2,26},{3,27},{4,28},{5,29},{6,30},{7,31},{8,16},{9,... | collective-permute-start | bytes 393224 | tf_op jit(solution)/shard_map/hh_gather/ppermute | solution.py:24
  24.4 31.2 %copy-start.1 = (bf16[4,192,256]{2,1,0:T(8,128)(2,1)}, bf16[4,192,256]{2,1,0:T(8,128)(2,1)S(1)}, u32[]{:S(2)}) copy-start(bf16[4,192,256]{2,1,0:T(8,128)(2,1)S(1)} %pad_maximum_fusion.refs_0_) | copy-start | bytes 1179652
  24.4 20.6 %collective-permute-start.6 = (bf16[4,192,256]{2,1,0:T(8,128)(2,1)S(1)}, bf16[4,192,256]{2,1,0:T(8,128)(2,1)S(1)}, u32[]{:S(2)}, u32[]{:S(2)}) collective-permute-start(bf16[4,192,256]{2,1,0:T(8,128)(2,1)S(1)} %pad_maximum_fusion.refs_0_), channel_id=1, source_target_pairs={{0,8},{1,9},{2,10},{3,11},{4,12},{5,13},{6,14},{7,15},{8,0},{9,1},... | collective-permute-start | bytes 1179656 | tf_op jit(solution)/shard_map/xy_gather/ppermute | solution.py:24
  25.0 21.5 %collective-permute-start.7 = (bf16[4,192,256]{2,1,0:T(8,128)(2,1)S(1)}, bf16[4,192,256]{2,1,0:T(8,128)(2,1)S(1)}, u32[]{:S(2)}, u32[]{:S(2)}) collective-permute-start(bf16[4,192,256]{2,1,0:T(8,128)(2,1)S(1)} %pad_maximum_fusion.refs_0_), channel_id=1, source_target_pairs={{0,16},{1,17},{2,18},{3,19},{4,20},{5,21},{6,22},{7,23},{8,24},{9,... | collective-permute-start | bytes 1179656 | tf_op jit(solution)/shard_map/xy_gather/ppermute | solution.py:24
  25.3 27.4 %collective-permute-start.10 = (bf16[4,192,256]{2,1,0:T(8,128)(2,1)S(1)}, bf16[4,192,256]{2,1,0:T(8,128)(2,1)S(1)}, u32[]{:S(2)}, u32[]{:S(2)}) collective-permute-start(bf16[4,192,256]{2,1,0:T(8,128)(2,1)S(1)} %pad_maximum_fusion.refs_0_), channel_id=1, source_target_pairs={{0,1},{1,0},{2,3},{3,2},{4,5},{5,4},{6,7},{7,6},{8,9},{9,8},{10,11... | collective-permute-start | bytes 1179656 | tf_op jit(solution)/shard_map/core_gather/ppermute | solution.py:24
  45.0 10.6 %copy-start.4 = (bf16[4,192,256]{2,1,0:T(8,128)(2,1)}, bf16[4,192,256]{2,1,0:T(8,128)(2,1)S(1)}, u32[]{:S(2)}) copy-start(bf16[4,192,256]{2,1,0:T(8,128)(2,1)S(1)} %collective-permute-done.6.refs_1_) | copy-start | bytes 1179652
  45.0 6.6 %collective-permute-start.8 = (bf16[2,192,256]{2,1,0:T(8,128)(2,1)S(1)}, bf16[2,192,256]{2,1,0:T(8,128)(2,1)S(1)}, u32[]{:S(2)}, u32[]{:S(2)}) collective-permute-start(bf16[2,192,256]{2,1,0:T(8,128)(2,1)S(1)} %slice.20), channel_id=1, source_target_pairs={{0,16},{1,17},{2,18},{3,19},{4,20},{5,21},{6,22},{7,23},{8,24},{9,... | collective-permute-start | bytes 589832 | tf_op jit(solution)/shard_map/xy_gather/ppermute | solution.py:24
  46.5 7.6 %copy-start.5 = (bf16[4,192,256]{2,1,0:T(8,128)(2,1)}, bf16[4,192,256]{2,1,0:T(8,128)(2,1)S(1)}, u32[]{:S(2)}) copy-start(bf16[4,192,256]{2,1,0:T(8,128)(2,1)S(1)} %collective-permute-done.7.refs_2_) | copy-start | bytes 1179652
  46.6 6.1 %collective-permute-start.9 = (bf16[2,192,256]{2,1,0:T(8,128)(2,1)S(1)}, bf16[2,192,256]{2,1,0:T(8,128)(2,1)S(1)}, u32[]{:S(2)}, u32[]{:S(2)}) collective-permute-start(bf16[2,192,256]{2,1,0:T(8,128)(2,1)S(1)} %slice.21), channel_id=1, source_target_pairs={{0,8},{1,9},{2,10},{3,11},{4,12},{5,13},{6,14},{7,15},{8,0},{9,1},... | collective-permute-start | bytes 589832 | tf_op jit(solution)/shard_map/xy_gather/ppermute | solution.py:24
  47.9 6.2 %collective-permute-start.11 = (bf16[4,192,256]{2,1,0:T(8,128)(2,1)S(1)}, bf16[4,192,256]{2,1,0:T(8,128)(2,1)S(1)}, u32[]{:S(2)}, u32[]{:S(2)}) collective-permute-start(bf16[4,192,256]{2,1,0:T(8,128)(2,1)S(1)} %collective-permute-done.6.refs_1_), channel_id=1, source_target_pairs={{0,1},{1,0},{2,3},{3,2},{4,5},{5,4},{6,7},{7,6},{8,9},{9,8},{10,11... | collective-permute-start | bytes 1179656 | tf_op jit(solution)/shard_map/core_gather/ppermute | solution.py:24
  48.0 7.6 %collective-permute-start.12 = (bf16[4,192,256]{2,1,0:T(8,128)(2,1)S(1)}, bf16[4,192,256]{2,1,0:T(8,128)(2,1)}, u32[]{:S(2)}, u32[]{:S(2)}) collective-permute-start(bf16[4,192,256]{2,1,0:T(8,128)(2,1)S(1)} %collective-permute-done.7.refs_2_), channel_id=1, source_target_pairs={{0,1},{1,0},{2,3},{3,2},{4,5},{5,4},{6,7},{7,6},{8,9},{9,8},{10,11... | collective-permute-start | bytes 1179656 | tf_op jit(solution)/shard_map/core_gather/ppermute | solution.py:24
  51.7 2.5 %copy-start.8 = (bf16[2,192,256]{2,1,0:T(8,128)(2,1)}, bf16[2,192,256]{2,1,0:T(8,128)(2,1)S(1)}, u32[]{:S(2)}) copy-start(bf16[2,192,256]{2,1,0:T(8,128)(2,1)S(1)} %collective-permute-done.8.refs_3_) | copy-start | bytes 589828
  51.7 1.4 %collective-permute-start.13 = (bf16[2,192,256]{2,1,0:T(8,128)(2,1)S(1)}, bf16[2,192,256]{2,1,0:T(8,128)(2,1)S(1)}, u32[]{:S(2)}, u32[]{:S(2)}) collective-permute-start(bf16[2,192,256]{2,1,0:T(8,128)(2,1)S(1)} %collective-permute-done.8.refs_3_), channel_id=1, source_target_pairs={{0,1},{1,0},{2,3},{3,2},{4,5},{5,4},{6,7},{7,6},{8,9},{9,8},{10,11... | collective-permute-start | bytes 589832 | tf_op jit(solution)/shard_map/core_gather/ppermute | solution.py:24
  52.7 1.4 %collective-permute-start.14 = (bf16[2,192,256]{2,1,0:T(8,128)(2,1)S(1)}, bf16[2,192,256]{2,1,0:T(8,128)(2,1)S(1)}, u32[]{:S(2)}, u32[]{:S(2)}) collective-permute-start(bf16[2,192,256]{2,1,0:T(8,128)(2,1)S(1)} %collective-permute-done.9.refs_4_), channel_id=1, source_target_pairs={{0,1},{1,0},{2,3},{3,2},{4,5},{5,4},{6,7},{7,6},{8,9},{9,8},{10,11... | collective-permute-start | bytes 589832 | tf_op jit(solution)/shard_map/core_gather/ppermute | solution.py:24
  52.7 21.0 %copy-start = (bf16[64,4096]{1,0:T(8,128)(2,1)}, bf16[64,4096]{1,0:T(8,128)(2,1)S(1)}, u32[]{:S(2)}) copy-start(bf16[64,4096]{1,0:T(8,128)(2,1)S(1)} %constant_dynamic-update-slice_fusion) | copy-start | bytes 1572868
  73.7 32.6 %all-to-all-start.1 = ((bf16[32,2,16,512]{3,2,1,0:T(8,128)(2,1)}), bf16[32,2,16,512]{3,2,1,0:T(8,128)(2,1)}, u32[]{:S(2)}, u32[]{:S(2)}) async-start(bf16[32,2,16,512]{3,2,1,0:T(8,128)(2,1)} %ladder.1), calls=%async_computation.1 | async-start | bytes 2097152 | tf_op jit(solution)/shard_map/pair_back/all_to_all | solution.py:161
  (7 other events, 8.4 us)
